TPU v7x, 32 devices: a whole 2x2x4 slice. The times are simulated.
32 devices in a mesh: tm: 2 (over core), loan: 8 (over z, y), cov: 2 (over x).
Axes of the slice: x: 2, y: 2, z: 4, core: 2. Of those that a mesh axis runs over, the one named last changes fastest.
Arguments:
- covars: float32 [65536, 1024], P(('tm', 'loan'), 'cov'), may hold values from -6 to 6
- events: int32 [65536], P(('tm', 'loan')), may hold values 0 or 1
- group: int32 [65536], P(('tm', 'loan')), may hold values from 0 to 511, as said below
- counts: int32 [16], P(('tm', 'loan')), may hold values from 1024 to 4096
- beta: float32 [1024], P('cov'), may hold values from -0.1875 to 0.1875
- vecs: float32 [2, 1024], P(None, 'cov'), may hold values from -12 to 12
Outputs:
- hessvec: float32 [2, 1024], P(None, 'cov')
Inputs may be any that keep to these rules, and one draw needn't show every extreme that they name: `group`: block b holds tie groups of time shard b // (16 // (512 // 256)) only: from 256 times the shard's index to 256 more minus one; the first 256 rows of every block hold each of these groups once.
All inputs are finite; a program needn't handle non-finite values. No bound on the sum of `events` on one device may be relied on, other than what follows from the above.
Results may differ from a plain program's by a relative error of at most 0.00028.
Values sent between devices are 32-bit elements; how exact they have to be, the bound alone decides.
No kernel may reach another device: no remote copies, remote signals or barrier semaphores. Data moves between devices by JAX's collectives and lax.ppermute only.
A program may use at most 64 MiB of HBM per device.

v0:
```python
import jax
import jax.numpy as jnp
from jax import lax
from jax.sharding import PartitionSpec as P

G_SH = 256


exact_mode = lax.Precision.HIGHEST


def carried_in(value, axis, join, neutral, backward):
    count, mine = (lax.axis_size(axis), lax.axis_index(axis))
    pieces = lax.all_gather(value, axis)
    if backward:
        pieces = pieces[::-1]
        mine = count - 1 - mine
    running = jnp.full_like(value, 0) + jnp.asarray(neutral, value.dtype)

    def hop(position, running):
        longer = join(running, pieces[position])
        return jnp.where(position < mine, longer, running)

    return lax.fori_loop(0, count - 1, hop, running)


def add_trees(earlier, later):
    return jax.tree.map(jnp.add, earlier, later)


def sweep(trips, block, update, initial):

    def advance(trip_index, carry):
        return update(trip_index * block, carry)

    return lax.fori_loop(0, trips, advance, initial)


def per_device(covars, events, group, counts, beta, vecs):
    row_total, col_width = covars.shape
    block = min(512, row_total)
    shard = lax.axis_index("tm")
    records_all = row_total * lax.axis_size("tm") * lax.axis_size("loan")
    row_count = counts[0]
    trips = row_total // block
    coeffs = jnp.concatenate([beta[None, :], vecs], axis=0)

    def predict(start, partial_value):
        piece = lax.dynamic_slice_in_dim(covars, start, block, 0)
        values = lax.dot_general(coeffs, piece, (((1,), (1,)), ((), ())), precision=exact_mode)
        return lax.dynamic_update_slice_in_dim(partial_value, values, start, 1)

    partial_value = sweep(trips, block, predict, jnp.zeros((3, row_total), jnp.float32))
    linear = lax.psum(partial_value, "cov")
    valid = (jnp.arange(row_total, dtype=jnp.int32) < row_count).astype(jnp.float32)
    weight = valid * jnp.exp(linear[0])
    projected = linear[1:3]
    died = valid * events.astype(jnp.float32)
    per_record = jnp.concatenate(
        [weight[None, :], weight[None, :] * projected, died[None, :]], axis=0
    )
    local_group = group - shard * G_SH
    group_iota = jnp.arange(G_SH, dtype=jnp.int32)
    upper_ones = (group_iota[:, None] >= group_iota[None, :]).astype(jnp.float32)

    def indicator(start):
        labels = lax.dynamic_slice_in_dim(local_group, start, block, 0)
        return (labels[:, None] == group_iota[None, :]).astype(jnp.float32)

    def tally(start, stats_acc):
        member = indicator(start)
        values = lax.dynamic_slice_in_dim(per_record, start, block, 1)
        return stats_acc + jnp.dot(values, member, precision=exact_mode)

    stats_local = sweep(trips, block, tally, jnp.zeros((4, G_SH), jnp.float32))
    totals = lax.psum(stats_local, "loan")
    sums = totals[:3]
    died_grp = totals[3]
    tail = carried_in(jnp.sum(sums, axis=1), "tm", add_trees, jnp.zeros((3,), jnp.float32), True)
    risk = jnp.dot(sums, upper_ones, precision=exact_mode) + tail[:, None]
    ratios = jnp.concatenate(
        [
            (died_grp / risk[0])[None, :],
            died_grp[None, :] * risk[1:3] / (risk[0] * risk[0])[None, :],
        ],
        axis=0,
    )
    head = carried_in(jnp.sum(ratios, axis=1), "tm", add_trees, jnp.zeros((3,), jnp.float32), False)
    cumulative = jnp.dot(ratios, upper_ones.T, precision=exact_mode) + head[:, None]

    def assemble(start, product_acc):
        member = indicator(start)
        looked = lax.dot_general(cumulative, member, (((1,), (1,)), ((), ())), precision=exact_mode)
        weight_part = lax.dynamic_slice_in_dim(weight, start, block, 0)
        proj_part = lax.dynamic_slice_in_dim(projected, start, block, 1)
        resid = weight_part[None, :] * (proj_part * looked[0][None, :] - looked[1:3])
        piece = lax.dynamic_slice_in_dim(covars, start, block, 0)
        return product_acc + jnp.dot(resid, piece, precision=exact_mode)

    parts = sweep(trips, block, assemble, jnp.zeros((2, col_width), jnp.float32))
    product = lax.psum(parts, ("tm", "loan"))
    return product / records_all


def solution(mesh):
    return jax.shard_map(
        per_device,
        mesh=mesh,
        in_specs=(
            P(("tm", "loan"), "cov"),
            P(("tm", "loan")),
            P(("tm", "loan")),
            P(("tm", "loan")),
            P("cov"),
            P(None, "cov"),
        ),
        out_specs=P(None, "cov"),
        check_vma=False,
    )
```

profile of v0, /device:TPU:0, one launch (start us, length us, event | category | flops | bytes accessed | tf_op | source)
XLA Modules:
  0.0 113.7 jit_solution(10290802062483819432)
XLA Ops:
  1.4 17.8 %while.51 = (s32[]{:T(128)}, f32[3,4096]{1,0:T(4,128)S(1)}, f32[4096,512]{1,0:T(8,128)}, f32[3,512]{1,0:T(4,128)S(1)}, s32[]{:T(128)}, /*index=5*/s32[]{:T(128)}, s32[]{:T(128)}, s32[]{:T(128)}) while((s32[]{:T(128)}, f32[3,4096]{1,0:T(4,128)S(1)}, f32[4096,512]{1,0:T(8,128)}, f32[3,512]{1,0:T(4,128)S(1)}, s32[]{:T(128)}, ...), condition=%wide.region_1.0_spmd, body=%wide.region_0.0_spmd.sunk | while | flops 9437190 | bytes 1066115 | solution.py:36
  1.4 2.2 %fusion.35 = f32[3,4096]{1,0:T(4,128)S(1)} fusion(f32[3,4096]{1,0:T(4,128)S(1)} %get-tuple-element.532, s32[]{:T(128)S(6)} %select_n.77, f32[3,512]{1,0:T(4,128)S(1)} %get-tuple-element.542, f32[4096,512]{1,0:T(8,128)} %get-tuple-element.541), kind=kOutput, calls=%fused_computation.3.clone.1 | convolution fusion | flops 9437184 | bytes 1065984 | tf_op jit(solution)/shard_map/while/body/eval_jaxpr/dot_general | solution.py:50
  3.6 2.2 %fusion.35 = f32[3,4096]{1,0:T(4,128)S(1)} fusion(f32[3,4096]{1,0:T(4,128)S(1)} %get-tuple-element.532, s32[]{:T(128)S(6)} %select_n.77, f32[3,512]{1,0:T(4,128)S(1)} %get-tuple-element.542, f32[4096,512]{1,0:T(8,128)} %get-tuple-element.541), kind=kOutput, calls=%fused_computation.3.clone.1 | convolution fusion | flops 9437184 | bytes 1065984 | tf_op jit(solution)/shard_map/while/body/eval_jaxpr/dot_general | solution.py:50
  5.8 2.2 %fusion.35 = f32[3,4096]{1,0:T(4,128)S(1)} fusion(f32[3,4096]{1,0:T(4,128)S(1)} %get-tuple-element.532, s32[]{:T(128)S(6)} %select_n.77, f32[3,512]{1,0:T(4,128)S(1)} %get-tuple-element.542, f32[4096,512]{1,0:T(8,128)} %get-tuple-element.541), kind=kOutput, calls=%fused_computation.3.clone.1 | convolution fusion | flops 9437184 | bytes 1065984 | tf_op jit(solution)/shard_map/while/body/eval_jaxpr/dot_general | solution.py:50
  8.0 2.2 %fusion.35 = f32[3,4096]{1,0:T(4,128)S(1)} fusion(f32[3,4096]{1,0:T(4,128)S(1)} %get-tuple-element.532, s32[]{:T(128)S(6)} %select_n.77, f32[3,512]{1,0:T(4,128)S(1)} %get-tuple-element.542, f32[4096,512]{1,0:T(8,128)} %get-tuple-element.541), kind=kOutput, calls=%fused_computation.3.clone.1 | convolution fusion | flops 9437184 | bytes 1065984 | tf_op jit(solution)/shard_map/while/body/eval_jaxpr/dot_general | solution.py:50
  10.3 2.2 %fusion.35 = f32[3,4096]{1,0:T(4,128)S(1)} fusion(f32[3,4096]{1,0:T(4,128)S(1)} %get-tuple-element.532, s32[]{:T(128)S(6)} %select_n.77, f32[3,512]{1,0:T(4,128)S(1)} %get-tuple-element.542, f32[4096,512]{1,0:T(8,128)} %get-tuple-element.541), kind=kOutput, calls=%fused_computation.3.clone.1 | convolution fusion | flops 9437184 | bytes 1065984 | tf_op jit(solution)/shard_map/while/body/eval_jaxpr/dot_general | solution.py:50
  12.5 2.2 %fusion.35 = f32[3,4096]{1,0:T(4,128)S(1)} fusion(f32[3,4096]{1,0:T(4,128)S(1)} %get-tuple-element.532, s32[]{:T(128)S(6)} %select_n.77, f32[3,512]{1,0:T(4,128)S(1)} %get-tuple-element.542, f32[4096,512]{1,0:T(8,128)} %get-tuple-element.541), kind=kOutput, calls=%fused_computation.3.clone.1 | convolution fusion | flops 9437184 | bytes 1065984 | tf_op jit(solution)/shard_map/while/body/eval_jaxpr/dot_general | solution.py:50
  14.7 2.2 %fusion.35 = f32[3,4096]{1,0:T(4,128)S(1)} fusion(f32[3,4096]{1,0:T(4,128)S(1)} %get-tuple-element.532, s32[]{:T(128)S(6)} %select_n.77, f32[3,512]{1,0:T(4,128)S(1)} %get-tuple-element.542, f32[4096,512]{1,0:T(8,128)} %get-tuple-element.541), kind=kOutput, calls=%fused_computation.3.clone.1 | convolution fusion | flops 9437184 | bytes 1065984 | tf_op jit(solution)/shard_map/while/body/eval_jaxpr/dot_general | solution.py:50
  16.9 2.2 %fusion.35 = f32[3,4096]{1,0:T(4,128)S(1)} fusion(f32[3,4096]{1,0:T(4,128)S(1)} %get-tuple-element.532, s32[]{:T(128)S(6)} %select_n.77, f32[3,512]{1,0:T(4,128)S(1)} %get-tuple-element.542, f32[4096,512]{1,0:T(8,128)} %get-tuple-element.541), kind=kOutput, calls=%fused_computation.3.clone.1 | convolution fusion | flops 9437184 | bytes 1065984 | tf_op jit(solution)/shard_map/while/body/eval_jaxpr/dot_general | solution.py:50
  19.1 10.4 %psum.21 = f32[3,4096]{1,0:T(4,128)S(1)} all-reduce(f32[3,4096]{1,0:T(4,128)S(1)} %get-tuple-element.347), channel_id=1, replica_groups=mesh['tm'=2,'loan'=8,'cov'=2] {'cov'}, use_global_device_ids=true, to_apply=%region_2.0 | all-reduce | flops 12288 | bytes 98304 | tf_op jit(solution)/shard_map/psum | solution.py:54
  31.2 3.3 %while.52 = (s32[]{:T(128)}, f32[4,256]{1,0:T(4,128)S(1)}, f32[4,4096]{1,0:T(4,128)S(1)}, s32[4096]{0:T(1024)S(1)}, s32[]{:T(128)}, /*index=5*/s32[]{:T(128)}, s32[]{:T(128)}, s32[]{:T(128)}) while((s32[]{:T(128)}, f32[4,256]{1,0:T(4,128)S(1)}, f32[4,4096]{1,0:T(4,128)S(1)}, s32[4096]{0:T(1024)S(1)}, s32[]{:T(128)}, ...), condition=%wide.region_4.0_spmd.clone, body=%wide.region_3.0_spmd.clone.sunk | while | flops 6424583 | bytes 22677 | solution.py:36
  34.5 21.6 %psum.22 = f32[4,256]{1,0:T(4,128)S(1)} all-reduce(f32[4,256]{1,0:T(4,128)S(1)} %get-tuple-element.348), channel_id=1, replica_groups=mesh['tm'=2,'loan'=8,'cov'=2] {'loan'}, use_global_device_ids=true, to_apply=%region_5.0 | all-reduce | flops 1024 | bytes 8192 | tf_op jit(solution)/shard_map/psum | solution.py:76
  58.5 2.4 %all-reduce = f32[6]{0:T(128)S(1)} all-reduce(f32[6]{0:T(128)S(1)} %dynamic-update-slice), channel_id=2, replica_groups=mesh['tm'=2,'loan'=8,'cov'=2] {'tm'}, use_global_device_ids=true, to_apply=%add | all-reduce | flops 6 | bytes 48
  61.6 2.4 %all-reduce.1 = f32[6]{0:T(128)S(1)} all-reduce(f32[6]{0:T(128)S(1)} %dynamic-update-slice.1), channel_id=3, replica_groups=mesh['tm'=2,'loan'=8,'cov'=2] {'tm'}, use_global_device_ids=true, to_apply=%add.1 | all-reduce | flops 6 | bytes 48
  64.3 19.3 %while.53 = (s32[]{:T(128)}, f32[2,512]{1,0:T(2,128)S(1)}, f32[4096]{0:T(1024)S(1)}, f32[2,4096]{1,0:T(2,128)S(1)}, s32[4096]{0:T(1024)S(1)}, /*index=5*/f32[3,2...) while((s32[]{:T(128)}, f32[2,512]{1,0:T(2,128)S(1)}, ...), condition=%wide.region_9.10_spmd.clone, body=%wide.region_8.9_spmd.clone.sunk | while | flops 11146247 | bytes 1094316 | solution.py:36
  64.9 1.9 %convolution_add_fusion.7 = f32[2,512]{1,0:T(2,128)S(1)} fusion(f32[4096,512]{1,0:T(8,128)} %get-tuple-element.599, s32[]{:T(128)S(6)} %select_n.79, f32[3,512]{1,0:T(4,128)S(1)} %convolution_bitcast_fusion.3, f32[2,512]{1,0:T(2,128)S(1)} %get-tuple-element.583, f32[2,4096]{1,0:T(2,128)S(1)} %get-tuple-element.596, pred[]{:T(512)S(6)} %compare.7, ...), kind=kOutput, calls=%fused_computation.12.clone.1 | convolution fusion | flops 6296576 | bytes 1070592 | tf_op jit(solution)/shard_map/while/body/eval_jaxpr/dot_general | solution.py:98
  67.3 1.9 %convolution_add_fusion.7 = f32[2,512]{1,0:T(2,128)S(1)} fusion(f32[4096,512]{1,0:T(8,128)} %get-tuple-element.599, s32[]{:T(128)S(6)} %select_n.79, f32[3,512]{1,0:T(4,128)S(1)} %convolution_bitcast_fusion.3, f32[2,512]{1,0:T(2,128)S(1)} %get-tuple-element.583, f32[2,4096]{1,0:T(2,128)S(1)} %get-tuple-element.596, pred[]{:T(512)S(6)} %compare.7, ...), kind=kOutput, calls=%fused_computation.12.clone.1 | convolution fusion | flops 6296576 | bytes 1070592 | tf_op jit(solution)/shard_map/while/body/eval_jaxpr/dot_general | solution.py:98
  69.7 1.9 %convolution_add_fusion.7 = f32[2,512]{1,0:T(2,128)S(1)} fusion(f32[4096,512]{1,0:T(8,128)} %get-tuple-element.599, s32[]{:T(128)S(6)} %select_n.79, f32[3,512]{1,0:T(4,128)S(1)} %convolution_bitcast_fusion.3, f32[2,512]{1,0:T(2,128)S(1)} %get-tuple-element.583, f32[2,4096]{1,0:T(2,128)S(1)} %get-tuple-element.596, pred[]{:T(512)S(6)} %compare.7, ...), kind=kOutput, calls=%fused_computation.12.clone.1 | convolution fusion | flops 6296576 | bytes 1070592 | tf_op jit(solution)/shard_map/while/body/eval_jaxpr/dot_general | solution.py:98
  72.1 1.9 %convolution_add_fusion.7 = f32[2,512]{1,0:T(2,128)S(1)} fusion(f32[4096,512]{1,0:T(8,128)} %get-tuple-element.599, s32[]{:T(128)S(6)} %select_n.79, f32[3,512]{1,0:T(4,128)S(1)} %convolution_bitcast_fusion.3, f32[2,512]{1,0:T(2,128)S(1)} %get-tuple-element.583, f32[2,4096]{1,0:T(2,128)S(1)} %get-tuple-element.596, pred[]{:T(512)S(6)} %compare.7, ...), kind=kOutput, calls=%fused_computation.12.clone.1 | convolution fusion | flops 6296576 | bytes 1070592 | tf_op jit(solution)/shard_map/while/body/eval_jaxpr/dot_general | solution.py:98
  74.5 1.9 %convolution_add_fusion.7 = f32[2,512]{1,0:T(2,128)S(1)} fusion(f32[4096,512]{1,0:T(8,128)} %get-tuple-element.599, s32[]{:T(128)S(6)} %select_n.79, f32[3,512]{1,0:T(4,128)S(1)} %convolution_bitcast_fusion.3, f32[2,512]{1,0:T(2,128)S(1)} %get-tuple-element.583, f32[2,4096]{1,0:T(2,128)S(1)} %get-tuple-element.596, pred[]{:T(512)S(6)} %compare.7, ...), kind=kOutput, calls=%fused_computation.12.clone.1 | convolution fusion | flops 6296576 | bytes 1070592 | tf_op jit(solution)/shard_map/while/body/eval_jaxpr/dot_general | solution.py:98
  76.9 1.9 %convolution_add_fusion.7 = f32[2,512]{1,0:T(2,128)S(1)} fusion(f32[4096,512]{1,0:T(8,128)} %get-tuple-element.599, s32[]{:T(128)S(6)} %select_n.79, f32[3,512]{1,0:T(4,128)S(1)} %convolution_bitcast_fusion.3, f32[2,512]{1,0:T(2,128)S(1)} %get-tuple-element.583, f32[2,4096]{1,0:T(2,128)S(1)} %get-tuple-element.596, pred[]{:T(512)S(6)} %compare.7, ...), kind=kOutput, calls=%fused_computation.12.clone.1 | convolution fusion | flops 6296576 | bytes 1070592 | tf_op jit(solution)/shard_map/while/body/eval_jaxpr/dot_general | solution.py:98
  79.3 1.9 %convolution_add_fusion.7 = f32[2,512]{1,0:T(2,128)S(1)} fusion(f32[4096,512]{1,0:T(8,128)} %get-tuple-element.599, s32[]{:T(128)S(6)} %select_n.79, f32[3,512]{1,0:T(4,128)S(1)} %convolution_bitcast_fusion.3, f32[2,512]{1,0:T(2,128)S(1)} %get-tuple-element.583, f32[2,4096]{1,0:T(2,128)S(1)} %get-tuple-element.596, pred[]{:T(512)S(6)} %compare.7, ...), kind=kOutput, calls=%fused_computation.12.clone.1 | convolution fusion | flops 6296576 | bytes 1070592 | tf_op jit(solution)/shard_map/while/body/eval_jaxpr/dot_general | solution.py:98
  81.7 1.9 %convolution_add_fusion.7 = f32[2,512]{1,0:T(2,128)S(1)} fusion(f32[4096,512]{1,0:T(8,128)} %get-tuple-element.599, s32[]{:T(128)S(6)} %select_n.79, f32[3,512]{1,0:T(4,128)S(1)} %convolution_bitcast_fusion.3, f32[2,512]{1,0:T(2,128)S(1)} %get-tuple-element.583, f32[2,4096]{1,0:T(2,128)S(1)} %get-tuple-element.596, pred[]{:T(512)S(6)} %compare.7, ...), kind=kOutput, calls=%fused_computation.12.clone.1 | convolution fusion | flops 6296576 | bytes 1070592 | tf_op jit(solution)/shard_map/while/body/eval_jaxpr/dot_general | solution.py:98
  83.6 29.5 %psum.23 = f32[2,512]{1,0:T(2,128)S(1)} all-reduce(f32[2,512]{1,0:T(2,128)S(1)} %get-tuple-element.349), channel_id=1, replica_groups=mesh['tm'=2,'loan'=8,'cov'=2] {'tm','loan'}, use_global_device_ids=true, to_apply=%region_10.11 | all-reduce | flops 1024 | bytes 8192 | tf_op jit(solution)/shard_map/psum | solution.py:101
  (72 shorter events, 13.2 us)
where the time goes:
time: 115 us; the launch traced here: 114 us
  blocking collectives  66.4 us (58%)
  matrix products  38.3 us (33%)
  local copies, waits for them, and re-layouts  4.14 us (4%)
  other arithmetic  3.32 us (3%)
  between operations  1.43 us (1%)
    psum x1, blocking collectives, per_device(): product = lax.psum(parts, ('tm', 'loan'))  29.5 us
    psum x1, blocking collectives, per_device(): totals = lax.psum(stats_local, 'loan')  21.6 us
    dot_general x8, matrix products, predict(): lax.dot_general(coeffs, piece, (((1,), (1,)), ((), ())), precision=exact_...  17.7 us
    dot_general x8, matrix products, assemble(): return product_acc + jnp.dot(resid, piece, precision=exact_mode)  14.8 us
    psum x1, blocking collectives, per_device(): linear = lax.psum(partial_value, 'cov')  10.4 us
    unnamed x2, blocking collectives  4.89 us
    dot_general x8, matrix products, assemble(): lax.dot_general(cumulative, member, (((1,), (1,)), ((), ())), precision=e...  2.98 us
    dot_general x8, matrix products, tally(): return stats_acc + jnp.dot(values, member, precision=exact_mode)  2.45 us

commit v1 on v0

v1 whole, which is shorter than its diff:
```python
import functools

import jax
import jax.numpy as jnp
from jax import lax
from jax.experimental import pallas as pl
from jax.experimental.pallas import tpu as pltpu
from jax.sharding import PartitionSpec as P

G_SH = 256
BF16 = jnp.bfloat16
F32 = jnp.float32


def split3(x):
    hi = x.astype(BF16).astype(F32)
    rest = x - hi
    mid = rest.astype(BF16).astype(F32)
    return hi, mid, rest - mid


def stack3(x):
    hi, mid, low = split3(x)
    return jnp.concatenate([hi, mid, low, jnp.zeros_like(x)], axis=0).astype(BF16)


def unstack3(y):
    return (y[16:24] + y[8:16]) + y[0:8]


def pad8(rows):
    width = rows[0].shape[1]
    used = sum(r.shape[0] for r in rows)
    return jnp.concatenate(list(rows) + [jnp.zeros((8 - used, width), F32)], axis=0)


def first_pass(
    chunk, covars, events, group, counts, shard, beta, vecs,
    lin, died, valid, member, high, low,
    buf, beta_v, vecs_v, group_v, events_v, count_s, shard_s, sems, small,
):
    rows = covars.shape[0]
    steps = rows // chunk
    copies = [
        pltpu.make_async_copy(group, group_v, small.at[0]),
        pltpu.make_async_copy(beta, beta_v, small.at[1]),
        pltpu.make_async_copy(vecs, vecs_v, small.at[2]),
        pltpu.make_async_copy(events, events_v, small.at[3]),
        pltpu.make_async_copy(counts, count_s, small.at[4]),
        pltpu.make_async_copy(shard, shard_s, small.at[5]),
    ]
    for copy in copies:
        copy.start()

    def piece(step):
        at = pl.ds(pl.multiple_of(step * chunk, chunk), chunk)
        return pltpu.make_async_copy(covars.at[at], buf.at[at], sems.at[step])

    for step in range(steps):
        piece(step).start()
    for copy in copies:
        copy.wait()
    index = lax.broadcasted_iota(jnp.int32, (1, rows), 1)
    ok = index < count_s[0]
    valid[...] = jnp.where(ok, 1.0, 0.0)
    died[...] = jnp.where(ok, events_v[...].astype(F32), 0.0)
    coeffs = stack3(pad8([beta_v[...], vecs_v[...]]))
    base = shard_s[0] * G_SH

    def body(step, carry):
        at = pl.ds(pl.multiple_of(step * chunk, chunk), chunk)
        labels = group_v[:, at] - base
        groups = lax.broadcasted_iota(jnp.int32, (G_SH, chunk), 0)
        member[:, at] = jnp.where(groups == labels, 1.0, 0.0).astype(BF16)
        piece(step).wait()
        full = buf[at, :]
        hi = full.astype(BF16)
        lo = (full - hi.astype(F32)).astype(BF16)
        high[at, :] = hi
        low[at, :] = lo
        dims = (((1,), (1,)), ((), ()))
        out = lax.dot_general(coeffs, hi, dims, preferred_element_type=F32)
        out += lax.dot_general(coeffs, lo, dims, preferred_element_type=F32)
        lin[:, at] = unstack3(out)[0:3]
        return carry

    lax.fori_loop(0, steps, body, 0)


def tally(mine, other, valid, died, member, stats, weighted):
    total = mine[...] + other[...]
    weight = jnp.where(valid[...] > 0.0, jnp.exp(total[0:1]), 0.0)
    proj = total[1:3]
    weighted[0:1] = weight
    weighted[1:3] = proj
    rows = pad8([weight, weight * proj, died[...]])
    out = lax.dot_general(
        stack3(rows), member[...], (((1,), (1,)), ((), ())), preferred_element_type=F32
    )
    sums = unstack3(out)[0:4]
    for slot in range(stats.shape[0]):
        stats[slot] = sums


def second_pass(shards, scale, shard, stats, weighted, member, high, low, out):
    me = shard[0]
    peers = stats.shape[0]
    each = peers // shards
    per_shard = []
    for s in range(shards):
        acc = stats[s * each]
        for p in range(1, each):
            acc = acc + stats[s * each + p]
        per_shard.append(acc)
    width = per_shard[0].shape[1]
    row = lax.broadcasted_iota(jnp.int32, (width, width), 0)
    col = lax.broadcasted_iota(jnp.int32, (width, width), 1)
    suffix = jnp.where(row >= col, 1.0, 0.0).astype(BF16)
    prefix = jnp.where(row <= col, 1.0, 0.0).astype(BF16)

    tail = jnp.zeros((4, 1), F32)
    tails = [None] * shards
    for s in reversed(range(shards)):
        tails[s] = tail
        tail = tail + jnp.sum(per_shard[s], axis=1, keepdims=True)

    def ratios_of(s):
        mat = stack3(pad8([per_shard[s]]))
        risk = unstack3(jnp.dot(mat, suffix, preferred_element_type=F32))[0:4] + tails[s]
        died_grp = per_shard[s][3:4]
        risk0 = risk[0:1]
        return pad8([died_grp / risk0, died_grp * risk[1:3] / (risk0 * risk0)])

    chosen = jnp.zeros((8, width), F32)
    head = jnp.zeros((8, 1), F32)
    for s in range(shards):
        value = ratios_of(s)
        chosen = jnp.where(me == s, value, chosen)
        head = head + jnp.where(me > s, jnp.sum(value, axis=1, keepdims=True), 0.0)
    cumulative = unstack3(jnp.dot(stack3(chosen), prefix, preferred_element_type=F32)) + head
    looked = unstack3(jnp.dot(stack3(cumulative), member[...], preferred_element_type=F32))
    weight = weighted[0:1]
    proj = weighted[1:3]
    resid = weight * (proj * looked[0:1] - looked[1:3])
    lhs = stack3(pad8([resid]))
    prod = jnp.dot(lhs, high[...], preferred_element_type=F32)
    prod += jnp.dot(lhs, low[...], preferred_element_type=F32)
    prod = unstack3(prod)[0:2] * scale
    for slot in range(out.shape[0]):
        out[slot] = prod


def per_device(covars, events, group, counts, beta, vecs):
    rows, cols = covars.shape
    shards = lax.axis_size("tm")
    peers = shards * lax.axis_size("loan")
    records = rows * peers
    chunk = min(512, rows)
    shard = lax.axis_index("tm").astype(jnp.int32)[None]
    hbm = pl.BlockSpec(memory_space=pltpu.HBM)
    vmem = pl.BlockSpec(memory_space=pltpu.VMEM)
    smem = pl.BlockSpec(memory_space=pltpu.SMEM)

    def arr(shape, dtype=F32):
        return jax.ShapeDtypeStruct(shape, dtype)

    def kept(shape, dtype=F32):
        return pltpu.VMEM(shape, dtype)

    lin, died, valid, member, high, low = pl.pallas_call(
        functools.partial(first_pass, chunk),
        out_shape=(
            arr((3, rows)), arr((1, rows)), arr((1, rows)),
            kept((G_SH, rows), BF16), kept((rows, cols), BF16), kept((rows, cols), BF16),
        ),
        in_specs=[hbm] * 7,
        out_specs=(vmem,) * 6,
        scratch_shapes=[
            pltpu.VMEM((rows, cols), F32),
            pltpu.VMEM((1, cols), F32),
            pltpu.VMEM((2, cols), F32),
            pltpu.VMEM((1, rows), jnp.int32),
            pltpu.VMEM((1, rows), jnp.int32),
            pltpu.SMEM((1,), jnp.int32),
            pltpu.SMEM((1,), jnp.int32),
            pltpu.SemaphoreType.DMA((rows // chunk,)),
            pltpu.SemaphoreType.DMA((6,)),
        ],
        compiler_params=pltpu.CompilerParams(vmem_limit_bytes=24 << 20),
        name="first_pass",
    )(covars, events[None], group[None], counts, shard, beta[None], vecs)

    pairs = [(i, i ^ 1) for i in range(2)]
    other = lax.ppermute(lin, "cov", pairs)

    stats, weighted = pl.pallas_call(
        tally,
        out_shape=(arr((peers, 4, G_SH)), arr((3, rows))),
        in_specs=[vmem] * 5,
        out_specs=(vmem,) * 2,
        compiler_params=pltpu.CompilerParams(vmem_limit_bytes=16 << 20),
        name="tally",
    )(lin, other, valid, died, member)

    everyone = lax.all_to_all(stats, ("tm", "loan"), 0, 0)

    parts = pl.pallas_call(
        functools.partial(second_pass, shards, 1.0 / records),
        out_shape=arr((peers, 2, cols)),
        in_specs=[smem] + [vmem] * 5,
        out_specs=vmem,
        compiler_params=pltpu.CompilerParams(vmem_limit_bytes=16 << 20),
        name="second_pass",
    )(shard, everyone, weighted, member, high, low)

    return jnp.sum(lax.all_to_all(parts, ("tm", "loan"), 0, 0), axis=0)


def solution(mesh):
    return jax.shard_map(
        per_device,
        mesh=mesh,
        in_specs=(
            P(("tm", "loan"), "cov"),
            P(("tm", "loan")),
            P(("tm", "loan")),
            P(("tm", "loan")),
            P("cov"),
            P(None, "cov"),
        ),
        out_specs=P(None, "cov"),
        check_vma=False,
    )
```

time: 115 us -> 43.2 us (0.38)
  blocking collectives: 66.4 us -> 22.3 us
  matrix products: 38.3 us -> 0 us
  Pallas kernels: 0 us -> 7.64 us
  starting transfers between devices: 0 us -> 3.03 us
  other arithmetic: 3.32 us -> 0.63 us
  waiting for transfers between devices: 0 us -> 2.25 us
  local copies, waits for them, and re-layouts: 4.14 us -> 6.18 us
    psum x3 -> x0, blocking collectives: 61.5 us -> none  [the longest x1 29.5 us: per_device(): product = lax.psum(parts, ('tm', 'loan'))]
    dot_general x34 -> x0, matrix products: 38.3 us -> none  [the longest x8 17.7 us: predict(): lax.dot_general(coeffs, piece, (((1,), (1,)), ((), ())), precision=exact_...]
    all_to_all x0 -> x2, blocking collectives: none -> 22.3 us  [the longest x1 13 us: per_device(): everyone = lax.all_to_all(stats, ('tm', 'loan'), 0, 0)]
    pallas_call x0 -> x3, Pallas kernels: none -> 7.64 us  [the longest x1 4.68 us: per_device(): pl.pallas_call(functools.partial(first_pass, chunk), out_shape=(arr((3, r...]
    unnamed x2 -> x0, blocking collectives: 4.89 us -> none
    unnamed x5 -> x10, local copies, waits for them, and re-layouts: 1.81 us -> 6.18 us
    ppermute x0 -> x1, starting transfers between devices: none -> 3.03 us  [per_device(): other = lax.ppermute(lin, 'cov', pairs)]
    dynamic_slice x24 -> x0, local copies, waits for them, and re-layouts: 2.28 us -> none  [the longest x16 1.47 us: indicator(): labels = lax.dynamic_slice_in_dim(local_group, start, block, 0)]
  transfers between devices with their start and end apart: 0 -> 1, of which waited for: 0 -> 1; matrix products, arithmetic and copies ran while one was open for 0% -> 0% of each run, Pallas kernels for 0% -> 0%
where the time goes in v1:
time: 43.2 us; the launch traced here: 42.7 us
  blocking collectives  22.3 us (52%)
  Pallas kernels  7.64 us (18%)
  local copies, waits for them, and re-layouts  6.18 us (14%)
  starting transfers between devices  3.03 us (7%)
  waiting for transfers between devices  2.25 us (5%)
  between operations  0.69 us (2%)
  other arithmetic  0.63 us (1%)
    all_to_all x1, blocking collectives, per_device(): everyone = lax.all_to_all(stats, ('tm', 'loan'), 0, 0)  13 us
    all_to_all x1, blocking collectives, per_device(): return jnp.sum(lax.all_to_all(parts, ('tm', 'loan'), 0, 0), axis=0)  9.31 us
    unnamed x10, local copies, waits for them, and re-layouts  6.18 us
    pallas_call x1, Pallas kernels, per_device(): pl.pallas_call(functools.partial(first_pass, chunk), out_shape=(arr((3, r...  4.68 us
    ppermute x1, starting transfers between devices, per_device(): other = lax.ppermute(lin, 'cov', pairs)  3.03 us
    ppermute x1, waiting for transfers between devices, per_device(): other = lax.ppermute(lin, 'cov', pairs)  2.25 us
    pallas_call x1, Pallas kernels, per_device(): pl.pallas_call(functools.partial(second_pass, shards, 1.0 / records), out...  2.23 us
  transfers between devices with their start and end apart: 1, of which 1 were waited for; matrix products, arithmetic and copies ran while one was open for 0% of the time, Pallas kernels for 0%

profile of v1, /device:TPU:0, one launch (start us, length us, event | category | flops | bytes accessed | tf_op | source)
XLA Modules:
  0.0 42.7 jit_solution(18258980547112880810)
XLA Ops:
  0.7 0.0 copy-start
  0.7 3.4 %copy-done = f32[4096,512]{1,0:T(8,128)S(1)} copy-done((f32[4096,512]{1,0:T(8,128)S(1)}, f32[4096,512]{1,0:T(8,128)}, u32[]{:S(2)}) %copy-start) | copy-done | bytes 8388632
  4.0 0.0 copy-start.1
  4.0 0.7 %copy-done.1 = s32[4096]{0:T(1024)S(1)} copy-done((s32[4096]{0:T(1024)S(1)}, s32[4096]{0:T(1024)}, u32[]{:S(2)}) %copy-start.1) | copy-done | bytes 16408
  4.8 0.0 copy-start.2
  4.8 0.7 %copy-done.2 = s32[4096]{0:T(1024)S(1)} copy-done((s32[4096]{0:T(1024)S(1)}, s32[4096]{0:T(1024)}, u32[]{:S(2)}) %copy-start.2) | copy-done | bytes 16408
  5.5 0.0 copy-start.3
  5.5 0.7 %copy-done.3 = f32[2,512]{1,0:T(2,128)S(1)} copy-done((f32[2,512]{1,0:T(2,128)S(1)}, f32[2,512]{1,0:T(2,128)}, u32[]{:S(2)}) %copy-start.3) | copy-done | bytes 4120
  6.2 0.0 copy-start.4
  6.2 0.7 %copy-done.4 = f32[512]{0:T(512)S(1)} copy-done((f32[512]{0:T(512)S(1)}, f32[512]{0:T(512)}, u32[]{:S(2)}) %copy-start.4) | copy-done | bytes 2072
  6.8 4.7 %first_pass.1 = (f32[3,4096]{1,0:T(4,128)S(1)}, f32[1,4096]{1,0:T(1,128)S(1)}, f32[1,4096]{1,0:T(1,128)S(1)}, bf16[256,4096]{1,0:T(8,128)(2,1)S(1)}, bf16[4096,5...) custom-call(f32[4096,512]{1,0:T(8,128)S(1)} %copy-done, s32[1,4096]{1,0:T(1,128)S(1)} %bitcast.4, ...), custom_call_target="tpu_custom_call" | custom-call | tf_op jit(solution)/shard_map/first_pass/pallas_call | solution.py:170
  11.5 3.0 %collective-permute-start = (f32[3,4096]{1,0:T(4,128)S(1)}, f32[3,4096]{1,0:T(4,128)S(1)}, u32[]{:S(2)}, u32[]{:S(2)}) collective-permute-start(f32[3,4096]{1,0:T(4,128)S(1)} %get-tuple-element.13.mine), channel_id=1, source_target_pairs={{0,1},{1,0},{2,3},{3,2},{4,5},{5,4},{6,7},{7,6},{8,9},{9,8},{10,11... | collective-permute-start | bytes 147464 | tf_op jit(solution)/shard_map/ppermute | solution.py:194
  14.6 2.2 %collective-permute-done.other = f32[3,4096]{1,0:T(4,128)S(1)} collective-permute-done((f32[3,4096]{1,0:T(4,128)S(1)}, f32[3,4096]{1,0:T(4,128)S(1)}, u32[]{:S(2)}, u32[]{:S(2)}) %collective-permute-start) | collective-permute-done | bytes 49184 | tf_op jit(solution)/shard_map/ppermute | solution.py:194
  16.8 0.7 %tally.1 = (f32[16,4,256]{2,1,0:T(4,128)S(1)}, f32[3,4096]{1,0:T(4,128)S(1)}) custom-call(f32[3,4096]{1,0:T(4,128)S(1)} %get-tuple-element.13.mine, f32[3,4096]{1,0:T(4,128)S(1)} %collective-permute-done.other, f32[1,4096]{1,0:T(1,128)S(1)} %get-tuple-element.14.valid, f32[1,4096]{1,0:T(1,128)S(1)} %get-tuple-element.15.died, ...), custom_call_target="tpu_custom_call" | custom-call | tf_op jit(solution)/shard_map/tally/pallas_call | solution.py:196
  17.6 13.0 %all_to_all.10.stats = f32[16,4,256]{2,1,0:T(4,128)S(1)} all-to-all(f32[16,4,256]{2,1,0:T(4,128)S(1)} %get-tuple-element.17), channel_id=1, replica_groups=mesh['tm'=2,'loan'=8,'cov'=2] {'tm','loan'}, dimensions={0} | all-to-all | bytes 131072 | tf_op jit(solution)/shard_map/all_to_all | solution.py:205
  30.6 2.2 %second_pass.1 = f32[16,2,512]{2,1,0:T(2,128)S(1)} custom-call(s32[1]{0:T(128)} %bitcast.shard, f32[16,4,256]{2,1,0:T(4,128)S(1)} %all_to_all.10.stats, f32[3,4096]{1,0:T(4,128)S(1)} %get-tuple-element.18.weighted, bf16[256,4096]{1,0:T(8,128)(2,1)S(1)} %get-tuple-element.16.member, bf16[4096,512]{1,0:T(8,128)(2,1)S(1)} %get-tuple-element.19.high, ...), custom_call_target="tpu_custom_call" | custom-call | tf_op jit(solution)/shard_map/second_pass/pallas_call | solution.py:207
  32.8 9.3 %all_to_all.11 = f32[16,2,512]{2,1,0:T(2,128)S(1)} all-to-all(f32[16,2,512]{2,1,0:T(2,128)S(1)} %second_pass.1), channel_id=1, replica_groups=mesh['tm'=2,'loan'=8,'cov'=2] {'tm','loan'}, dimensions={0} | all-to-all | bytes 131072 | tf_op jit(solution)/shard_map/all_to_all | solution.py:216
  42.1 0.6 %reduce_sum.9 = f32[2,512]{1,0:T(2,128)} reduce(f32[16,2,512]{2,1,0:T(2,128)S(1)} %all_to_all.11, f32[]{:T(128)} %constant.7.clone.1), dimensions={0}, to_apply=%region_0.0 | reduce | flops 15360 | bytes 69636 | tf_op jit(solution)/shard_map/reduce_sum | solution.py:216
Async XLA Ops:
  0.7 3.4 %copy-start = (f32[4096,512]{1,0:T(8,128)S(1)}, f32[4096,512]{1,0:T(8,128)}, u32[]{:S(2)}) copy-start(f32[4096,512]{1,0:T(8,128)} %covars.1) | copy-start | bytes 25165828
  4.0 0.7 %copy-start.1 = (s32[4096]{0:T(1024)S(1)}, s32[4096]{0:T(1024)}, u32[]{:S(2)}) copy-start(s32[4096]{0:T(1024)} %param.7) | copy-start | bytes 49156
  4.8 0.7 %copy-start.2 = (s32[4096]{0:T(1024)S(1)}, s32[4096]{0:T(1024)}, u32[]{:S(2)}) copy-start(s32[4096]{0:T(1024)} %param.8) | copy-start | bytes 49156
  5.5 0.7 %copy-start.3 = (f32[2,512]{1,0:T(2,128)S(1)}, f32[2,512]{1,0:T(2,128)}, u32[]{:S(2)}) copy-start(f32[2,512]{1,0:T(2,128)} %vecs.1) | copy-start | bytes 12292
  6.2 0.7 %copy-start.4 = (f32[512]{0:T(512)S(1)}, f32[512]{0:T(512)}, u32[]{:S(2)}) copy-start(f32[512]{0:T(512)} %param.10) | copy-start | bytes 6148
  11.5 5.3 %collective-permute-start = (f32[3,4096]{1,0:T(4,128)S(1)}, f32[3,4096]{1,0:T(4,128)S(1)}, u32[]{:S(2)}, u32[]{:S(2)}) collective-permute-start(f32[3,4096]{1,0:T(4,128)S(1)} %get-tuple-element.13.mine), channel_id=1, source_target_pairs={{0,1},{1,0},{2,3},{3,2},{4,5},{5,4},{6,7},{7,6},{8,9},{9,8},{10,11... | collective-permute-start | bytes 147464 | tf_op jit(solution)/shard_map/ppermute | solution.py:194

commit v2 on v1

--- a/solution.py
+++ b/solution.py
@@ -37,7 +37,7 @@
 def first_pass(
     chunk, covars, events, group, counts, shard, beta, vecs,
     lin, died, valid, member, high, low,
-    buf, beta_v, vecs_v, group_v, events_v, count_s, shard_s, sems, small,
+    buf, beta_v, vecs_v, group_v, events_v, sems, small,
 ):
     rows = covars.shape[0]
     steps = rows // chunk
@@ -46,8 +46,6 @@
         pltpu.make_async_copy(beta, beta_v, small.at[1]),
         pltpu.make_async_copy(vecs, vecs_v, small.at[2]),
         pltpu.make_async_copy(events, events_v, small.at[3]),
-        pltpu.make_async_copy(counts, count_s, small.at[4]),
-        pltpu.make_async_copy(shard, shard_s, small.at[5]),
     ]
     for copy in copies:
         copy.start()
@@ -61,11 +59,11 @@
     for copy in copies:
         copy.wait()
     index = lax.broadcasted_iota(jnp.int32, (1, rows), 1)
-    ok = index < count_s[0]
+    ok = index < counts[0]
     valid[...] = jnp.where(ok, 1.0, 0.0)
     died[...] = jnp.where(ok, events_v[...].astype(F32), 0.0)
     coeffs = stack3(pad8([beta_v[...], vecs_v[...]]))
-    base = shard_s[0] * G_SH
+    base = shard[0] * G_SH
 
     def body(step, carry):
         at = pl.ds(pl.multiple_of(step * chunk, chunk), chunk)
@@ -173,7 +171,7 @@
             arr((3, rows)), arr((1, rows)), arr((1, rows)),
             kept((G_SH, rows), BF16), kept((rows, cols), BF16), kept((rows, cols), BF16),
         ),
-        in_specs=[hbm] * 7,
+        in_specs=[hbm] * 3 + [smem] * 2 + [hbm] * 2,
         out_specs=(vmem,) * 6,
         scratch_shapes=[
             pltpu.VMEM((rows, cols), F32),
@@ -181,14 +179,20 @@
             pltpu.VMEM((2, cols), F32),
             pltpu.VMEM((1, rows), jnp.int32),
             pltpu.VMEM((1, rows), jnp.int32),
-            pltpu.SMEM((1,), jnp.int32),
-            pltpu.SMEM((1,), jnp.int32),
             pltpu.SemaphoreType.DMA((rows // chunk,)),
-            pltpu.SemaphoreType.DMA((6,)),
+            pltpu.SemaphoreType.DMA((4,)),
         ],
         compiler_params=pltpu.CompilerParams(vmem_limit_bytes=24 << 20),
         name="first_pass",
-    )(covars, events[None], group[None], counts, shard, beta[None], vecs)
+    )(
+        *(
+            pltpu.with_memory_space_constraint(x, pltpu.HBM)
+            for x in (covars, events[None], group[None])
+        ),
+        counts,
+        shard,
+        *(pltpu.with_memory_space_constraint(x, pltpu.HBM) for x in (beta[None], vecs)),
+    )
 
     pairs = [(i, i ^ 1) for i in range(2)]
     other = lax.ppermute(lin, "cov", pairs)

time: 43.2 us -> 39.1 us (0.905)
  local copies, waits for them, and re-layouts: 6.18 us -> 0 us
  Pallas kernels: 7.64 us -> 9.94 us
    unnamed x10 -> x0, local copies, waits for them, and re-layouts: 6.18 us -> none
    pallas_call x1, Pallas kernels: 4.68 us -> 6.97 us  [per_device(): pl.pallas_call(functools.partial(first_pass, chunk), out_shape=(arr((3, r...]
where the time goes in v2:
time: 39.1 us; the launch traced here: 38.9 us
  blocking collectives  22.3 us (57%)
  Pallas kernels  9.94 us (25%)
  starting transfers between devices  3.03 us (8%)
  waiting for transfers between devices  2.25 us (6%)
  between operations  0.68 us (2%)
  other arithmetic  0.63 us (2%)
    all_to_all x1, blocking collectives, per_device(): everyone = lax.all_to_all(stats, ('tm', 'loan'), 0, 0)  13 us
    all_to_all x1, blocking collectives, per_device(): return jnp.sum(lax.all_to_all(parts, ('tm', 'loan'), 0, 0), axis=0)  9.31 us
    pallas_call x1, Pallas kernels, per_device(): pl.pallas_call(functools.partial(first_pass, chunk), out_shape=(arr((3, r...  6.97 us
    ppermute x1, starting transfers between devices, per_device(): other = lax.ppermute(lin, 'cov', pairs)  3.03 us
    ppermute x1, waiting for transfers between devices, per_device(): other = lax.ppermute(lin, 'cov', pairs)  2.25 us
    pallas_call x1, Pallas kernels, per_device(): pl.pallas_call(functools.partial(second_pass, shards, 1.0 / records), out...  2.23 us
  transfers between devices with their start and end apart: 1, of which 1 were waited for; matrix products, arithmetic and copies ran while one was open for 0% of the time, Pallas kernels for 0%

profile of v2, /device:TPU:0, one launch (start us, length us, event | category | flops | bytes accessed | tf_op | source)
XLA Modules:
  0.0 38.9 jit_solution(11470035500144451346)
XLA Ops:
  0.7 7.0 %first_pass.1 = (f32[3,4096]{1,0:T(4,128)S(1)}, f32[1,4096]{1,0:T(1,128)S(1)}, f32[1,4096]{1,0:T(1,128)S(1)}, bf16[256,4096]{1,0:T(8,128)(2,1)S(1)}, bf16[4096,5...) custom-call(f32[4096,512]{1,0:T(8,128)} %covars.1, s32[1,4096]{1,0:T(1,128)} %bitcast.4, s32[1,4096]{1,0:T(1,128)} %bitcast.5, ...), custom_call_target="tpu_custom_call" | custom-call | tf_op jit(solution)/shard_map/first_pass/pallas_call | solution.py:168
  7.6 3.0 %collective-permute-start = (f32[3,4096]{1,0:T(4,128)S(1)}, f32[3,4096]{1,0:T(4,128)S(1)}, u32[]{:S(2)}, u32[]{:S(2)}) collective-permute-start(f32[3,4096]{1,0:T(4,128)S(1)} %get-tuple-element.13.mine), channel_id=1, source_target_pairs={{0,1},{1,0},{2,3},{3,2},{4,5},{5,4},{6,7},{7,6},{8,9},{9,8},{10,11... | collective-permute-start | bytes 147464 | tf_op jit(solution)/shard_map/ppermute | solution.py:198
  10.7 2.2 %collective-permute-done.other = f32[3,4096]{1,0:T(4,128)S(1)} collective-permute-done((f32[3,4096]{1,0:T(4,128)S(1)}, f32[3,4096]{1,0:T(4,128)S(1)}, u32[]{:S(2)}, u32[]{:S(2)}) %collective-permute-start) | collective-permute-done | bytes 49184 | tf_op jit(solution)/shard_map/ppermute | solution.py:198
  12.9 0.7 %tally.1 = (f32[16,4,256]{2,1,0:T(4,128)S(1)}, f32[3,4096]{1,0:T(4,128)S(1)}) custom-call(f32[3,4096]{1,0:T(4,128)S(1)} %get-tuple-element.13.mine, f32[3,4096]{1,0:T(4,128)S(1)} %collective-permute-done.other, f32[1,4096]{1,0:T(1,128)S(1)} %get-tuple-element.14.valid, f32[1,4096]{1,0:T(1,128)S(1)} %get-tuple-element.15.died, ...), custom_call_target="tpu_custom_call" | custom-call | tf_op jit(solution)/shard_map/tally/pallas_call | solution.py:200
  13.7 13.0 %all_to_all.10.stats = f32[16,4,256]{2,1,0:T(4,128)S(1)} all-to-all(f32[16,4,256]{2,1,0:T(4,128)S(1)} %get-tuple-element.17), channel_id=1, replica_groups=mesh['tm'=2,'loan'=8,'cov'=2] {'tm','loan'}, dimensions={0} | all-to-all | bytes 131072 | tf_op jit(solution)/shard_map/all_to_all | solution.py:209
  26.7 2.2 %second_pass.1 = f32[16,2,512]{2,1,0:T(2,128)S(1)} custom-call(s32[1]{0:T(128)} %bitcast.shard, f32[16,4,256]{2,1,0:T(4,128)S(1)} %all_to_all.10.stats, f32[3,4096]{1,0:T(4,128)S(1)} %get-tuple-element.18.weighted, bf16[256,4096]{1,0:T(8,128)(2,1)S(1)} %get-tuple-element.16.member, bf16[4096,512]{1,0:T(8,128)(2,1)S(1)} %get-tuple-element.19.high, ...), custom_call_target="tpu_custom_call" | custom-call | tf_op jit(solution)/shard_map/second_pass/pallas_call | solution.py:211
  28.9 9.3 %all_to_all.11 = f32[16,2,512]{2,1,0:T(2,128)S(1)} all-to-all(f32[16,2,512]{2,1,0:T(2,128)S(1)} %second_pass.1), channel_id=1, replica_groups=mesh['tm'=2,'loan'=8,'cov'=2] {'tm','loan'}, dimensions={0} | all-to-all | bytes 131072 | tf_op jit(solution)/shard_map/all_to_all | solution.py:220
  38.2 0.6 %reduce_sum.9 = f32[2,512]{1,0:T(2,128)} reduce(f32[16,2,512]{2,1,0:T(2,128)S(1)} %all_to_all.11, f32[]{:T(128)} %constant.7.clone.1), dimensions={0}, to_apply=%region_0.0 | reduce | flops 15360 | bytes 69636 | tf_op jit(solution)/shard_map/reduce_sum | solution.py:220
Async XLA Ops:
  7.6 5.3 %collective-permute-start = (f32[3,4096]{1,0:T(4,128)S(1)}, f32[3,4096]{1,0:T(4,128)S(1)}, u32[]{:S(2)}, u32[]{:S(2)}) collective-permute-start(f32[3,4096]{1,0:T(4,128)S(1)} %get-tuple-element.13.mine), channel_id=1, source_target_pairs={{0,1},{1,0},{2,3},{3,2},{4,5},{5,4},{6,7},{7,6},{8,9},{9,8},{10,11... | collective-permute-start | bytes 147464 | tf_op jit(solution)/shard_map/ppermute | solution.py:198

commit v3 on v2

--- a/solution.py
+++ b/solution.py
@@ -54,8 +54,9 @@
         at = pl.ds(pl.multiple_of(step * chunk, chunk), chunk)
         return pltpu.make_async_copy(covars.at[at], buf.at[at], sems.at[step])
 
-    for step in range(steps):
-        piece(step).start()
+    piece(0).start()
+    if steps > 1:
+        piece(1).start()
     for copy in copies:
         copy.wait()
     index = lax.broadcasted_iota(jnp.int32, (1, rows), 1)
@@ -64,13 +65,27 @@
     died[...] = jnp.where(ok, events_v[...].astype(F32), 0.0)
     coeffs = stack3(pad8([beta_v[...], vecs_v[...]]))
     base = shard[0] * G_SH
+    part = min(512, chunk)
+
+    def mark(step, carry):
+        at = pl.ds(pl.multiple_of(step * part, part), part)
+        labels = (group_v[:, at] - base).astype(F32).astype(BF16)
+        groups = lax.broadcasted_iota(jnp.int32, (G_SH, part), 0).astype(F32).astype(BF16)
+        member[:, at] = jnp.where(groups == labels, jnp.ones((), BF16), jnp.zeros((), BF16))
+        return carry
+
+    lax.fori_loop(0, rows // part, mark, 0)
+    if steps > 2:
+        piece(2).start()
 
     def body(step, carry):
         at = pl.ds(pl.multiple_of(step * chunk, chunk), chunk)
-        labels = group_v[:, at] - base
-        groups = lax.broadcasted_iota(jnp.int32, (G_SH, chunk), 0)
-        member[:, at] = jnp.where(groups == labels, 1.0, 0.0).astype(BF16)
         piece(step).wait()
+
+        @pl.when(step + 3 < steps)
+        def _():
+            piece(step + 3).start()
+
         full = buf[at, :]
         hi = full.astype(BF16)
         lo = (full - hi.astype(F32)).astype(BF16)
@@ -153,7 +168,7 @@
     shards = lax.axis_size("tm")
     peers = shards * lax.axis_size("loan")
     records = rows * peers
-    chunk = min(512, rows)
+    chunk = min(1024, rows)
     shard = lax.axis_index("tm").astype(jnp.int32)[None]
     hbm = pl.BlockSpec(memory_space=pltpu.HBM)
     vmem = pl.BlockSpec(memory_space=pltpu.VMEM)

time: 39.1 us -> 37.2 us (0.951)
  Pallas kernels: 9.94 us -> 8.01 us
    pallas_call x1, Pallas kernels: 6.97 us -> 5.05 us  [per_device(): pl.pallas_call(functools.partial(first_pass, chunk), out_shape=(arr((3, r...]
where the time goes in v3:
time: 37.2 us; the launch traced here: 36.9 us
  blocking collectives  22.3 us (60%)
  Pallas kernels  8.01 us (22%)
  starting transfers between devices  3.03 us (8%)
  waiting for transfers between devices  2.25 us (6%)
  between operations  0.68 us (2%)
  other arithmetic  0.63 us (2%)
    all_to_all x1, blocking collectives, per_device(): everyone = lax.all_to_all(stats, ('tm', 'loan'), 0, 0)  13 us
    all_to_all x1, blocking collectives, per_device(): return jnp.sum(lax.all_to_all(parts, ('tm', 'loan'), 0, 0), axis=0)  9.31 us
    pallas_call x1, Pallas kernels, per_device(): pl.pallas_call(functools.partial(first_pass, chunk), out_shape=(arr((3, r...  5.05 us
    ppermute x1, starting transfers between devices, per_device(): other = lax.ppermute(lin, 'cov', pairs)  3.03 us
    ppermute x1, waiting for transfers between devices, per_device(): other = lax.ppermute(lin, 'cov', pairs)  2.25 us
    pallas_call x1, Pallas kernels, per_device(): pl.pallas_call(functools.partial(second_pass, shards, 1.0 / records), out...  2.23 us
  transfers between devices with their start and end apart: 1, of which 1 were waited for; matrix products, arithmetic and copies ran while one was open for 0% of the time, Pallas kernels for 0%

profile of v3, /device:TPU:0, one launch (start us, length us, event | category | flops | bytes accessed | tf_op | source)
XLA Modules:
  0.0 36.9 jit_solution(7974931101469317595)
XLA Ops:
  0.7 5.0 %first_pass.1 = (f32[3,4096]{1,0:T(4,128)S(1)}, f32[1,4096]{1,0:T(1,128)S(1)}, f32[1,4096]{1,0:T(1,128)S(1)}, bf16[256,4096]{1,0:T(8,128)(2,1)S(1)}, bf16[4096,5...) custom-call(f32[4096,512]{1,0:T(8,128)} %covars.1, s32[1,4096]{1,0:T(1,128)} %bitcast.4, s32[1,4096]{1,0:T(1,128)} %bitcast.5, ...), custom_call_target="tpu_custom_call" | custom-call | tf_op jit(solution)/shard_map/first_pass/pallas_call | solution.py:183
  5.7 3.0 %collective-permute-start = (f32[3,4096]{1,0:T(4,128)S(1)}, f32[3,4096]{1,0:T(4,128)S(1)}, u32[]{:S(2)}, u32[]{:S(2)}) collective-permute-start(f32[3,4096]{1,0:T(4,128)S(1)} %get-tuple-element.13.mine), channel_id=1, source_target_pairs={{0,1},{1,0},{2,3},{3,2},{4,5},{5,4},{6,7},{7,6},{8,9},{9,8},{10,11... | collective-permute-start | bytes 147464 | tf_op jit(solution)/shard_map/ppermute | solution.py:213
  8.7 2.2 %collective-permute-done.other = f32[3,4096]{1,0:T(4,128)S(1)} collective-permute-done((f32[3,4096]{1,0:T(4,128)S(1)}, f32[3,4096]{1,0:T(4,128)S(1)}, u32[]{:S(2)}, u32[]{:S(2)}) %collective-permute-start) | collective-permute-done | bytes 49184 | tf_op jit(solution)/shard_map/ppermute | solution.py:213
  11.0 0.7 %tally.1 = (f32[16,4,256]{2,1,0:T(4,128)S(1)}, f32[3,4096]{1,0:T(4,128)S(1)}) custom-call(f32[3,4096]{1,0:T(4,128)S(1)} %get-tuple-element.13.mine, f32[3,4096]{1,0:T(4,128)S(1)} %collective-permute-done.other, f32[1,4096]{1,0:T(1,128)S(1)} %get-tuple-element.14.valid, f32[1,4096]{1,0:T(1,128)S(1)} %get-tuple-element.15.died, ...), custom_call_target="tpu_custom_call" | custom-call | tf_op jit(solution)/shard_map/tally/pallas_call | solution.py:215
  11.7 13.0 %all_to_all.10.stats = f32[16,4,256]{2,1,0:T(4,128)S(1)} all-to-all(f32[16,4,256]{2,1,0:T(4,128)S(1)} %get-tuple-element.17), channel_id=1, replica_groups=mesh['tm'=2,'loan'=8,'cov'=2] {'tm','loan'}, dimensions={0} | all-to-all | bytes 131072 | tf_op jit(solution)/shard_map/all_to_all | solution.py:224
  24.8 2.2 %second_pass.1 = f32[16,2,512]{2,1,0:T(2,128)S(1)} custom-call(s32[1]{0:T(128)} %bitcast.shard, f32[16,4,256]{2,1,0:T(4,128)S(1)} %all_to_all.10.stats, f32[3,4096]{1,0:T(4,128)S(1)} %get-tuple-element.18.weighted, bf16[256,4096]{1,0:T(8,128)(2,1)S(1)} %get-tuple-element.16.member, bf16[4096,512]{1,0:T(8,128)(2,1)S(1)} %get-tuple-element.19.high, ...), custom_call_target="tpu_custom_call" | custom-call | tf_op jit(solution)/shard_map/second_pass/pallas_call | solution.py:226
  27.0 9.3 %all_to_all.11 = f32[16,2,512]{2,1,0:T(2,128)S(1)} all-to-all(f32[16,2,512]{2,1,0:T(2,128)S(1)} %second_pass.1), channel_id=1, replica_groups=mesh['tm'=2,'loan'=8,'cov'=2] {'tm','loan'}, dimensions={0} | all-to-all | bytes 131072 | tf_op jit(solution)/shard_map/all_to_all | solution.py:235
  36.3 0.6 %reduce_sum.9 = f32[2,512]{1,0:T(2,128)} reduce(f32[16,2,512]{2,1,0:T(2,128)S(1)} %all_to_all.11, f32[]{:T(128)} %constant.7.clone.1), dimensions={0}, to_apply=%region_0.0 | reduce | flops 15360 | bytes 69636 | tf_op jit(solution)/shard_map/reduce_sum | solution.py:235
Async XLA Ops:
  5.7 5.3 %collective-permute-start = (f32[3,4096]{1,0:T(4,128)S(1)}, f32[3,4096]{1,0:T(4,128)S(1)}, u32[]{:S(2)}, u32[]{:S(2)}) collective-permute-start(f32[3,4096]{1,0:T(4,128)S(1)} %get-tuple-element.13.mine), channel_id=1, source_target_pairs={{0,1},{1,0},{2,3},{3,2},{4,5},{5,4},{6,7},{7,6},{8,9},{9,8},{10,11... | collective-permute-start | bytes 147464 | tf_op jit(solution)/shard_map/ppermute | solution.py:213

commit v4 on v3

--- a/solution.py
+++ b/solution.py
@@ -36,7 +36,7 @@
 
 def first_pass(
     chunk, covars, events, group, counts, shard, beta, vecs,
-    lin, died, valid, member, high, low,
+    lin, died, valid, reach, high, low,
     buf, beta_v, vecs_v, group_v, events_v, sems, small,
 ):
     rows = covars.shape[0]
@@ -71,7 +71,7 @@
         at = pl.ds(pl.multiple_of(step * part, part), part)
         labels = (group_v[:, at] - base).astype(F32).astype(BF16)
         groups = lax.broadcasted_iota(jnp.int32, (G_SH, part), 0).astype(F32).astype(BF16)
-        member[:, at] = jnp.where(groups == labels, jnp.ones((), BF16), jnp.zeros((), BF16))
+        reach[:, at] = jnp.where(groups <= labels, jnp.ones((), BF16), jnp.zeros((), BF16))
         return carry
 
     lax.fori_loop(0, rows // part, mark, 0)
@@ -100,7 +100,7 @@
     lax.fori_loop(0, steps, body, 0)
 
 
-def tally(mine, other, valid, died, member, stats, weighted):
+def tally(mine, other, valid, died, reach, stats, weighted):
     total = mine[...] + other[...]
     weight = jnp.where(valid[...] > 0.0, jnp.exp(total[0:1]), 0.0)
     proj = total[1:3]
@@ -108,14 +108,14 @@
     weighted[1:3] = proj
     rows = pad8([weight, weight * proj, died[...]])
     out = lax.dot_general(
-        stack3(rows), member[...], (((1,), (1,)), ((), ())), preferred_element_type=F32
+        stack3(rows), reach[...], (((1,), (1,)), ((), ())), preferred_element_type=F32
     )
     sums = unstack3(out)[0:4]
     for slot in range(stats.shape[0]):
         stats[slot] = sums
 
 
-def second_pass(shards, scale, shard, stats, weighted, member, high, low, out):
+def second_pass(shards, scale, shard, stats, weighted, reach, high, low, out):
     me = shard[0]
     peers = stats.shape[0]
     each = peers // shards
@@ -126,21 +126,18 @@
             acc = acc + stats[s * each + p]
         per_shard.append(acc)
     width = per_shard[0].shape[1]
-    row = lax.broadcasted_iota(jnp.int32, (width, width), 0)
-    col = lax.broadcasted_iota(jnp.int32, (width, width), 1)
-    suffix = jnp.where(row >= col, 1.0, 0.0).astype(BF16)
-    prefix = jnp.where(row <= col, 1.0, 0.0).astype(BF16)
+    lane = lax.broadcasted_iota(jnp.int32, (1, width), 1)
 
     tail = jnp.zeros((4, 1), F32)
     tails = [None] * shards
     for s in reversed(range(shards)):
         tails[s] = tail
-        tail = tail + jnp.sum(per_shard[s], axis=1, keepdims=True)
+        tail = tail + per_shard[s][:, 0:1]
 
     def ratios_of(s):
-        mat = stack3(pad8([per_shard[s]]))
-        risk = unstack3(jnp.dot(mat, suffix, preferred_element_type=F32))[0:4] + tails[s]
-        died_grp = per_shard[s][3:4]
+        risk = per_shard[s] + tails[s]
+        late = per_shard[s][3:4]
+        died_grp = late - jnp.where(lane == width - 1, 0.0, pltpu.roll(late, width - 1, 1))
         risk0 = risk[0:1]
         return pad8([died_grp / risk0, died_grp * risk[1:3] / (risk0 * risk0)])
 
@@ -150,8 +147,7 @@
         value = ratios_of(s)
         chosen = jnp.where(me == s, value, chosen)
         head = head + jnp.where(me > s, jnp.sum(value, axis=1, keepdims=True), 0.0)
-    cumulative = unstack3(jnp.dot(stack3(chosen), prefix, preferred_element_type=F32)) + head
-    looked = unstack3(jnp.dot(stack3(cumulative), member[...], preferred_element_type=F32))
+    looked = unstack3(jnp.dot(stack3(chosen), reach[...], preferred_element_type=F32)) + head
     weight = weighted[0:1]
     proj = weighted[1:3]
     resid = weight * (proj * looked[0:1] - looked[1:3])
@@ -180,7 +176,7 @@
     def kept(shape, dtype=F32):
         return pltpu.VMEM(shape, dtype)
 
-    lin, died, valid, member, high, low = pl.pallas_call(
+    lin, died, valid, reach, high, low = pl.pallas_call(
         functools.partial(first_pass, chunk),
         out_shape=(
             arr((3, rows)), arr((1, rows)), arr((1, rows)),
@@ -219,7 +215,7 @@
         out_specs=(vmem,) * 2,
         compiler_params=pltpu.CompilerParams(vmem_limit_bytes=16 << 20),
         name="tally",
-    )(lin, other, valid, died, member)
+    )(lin, other, valid, died, reach)
 
     everyone = lax.all_to_all(stats, ("tm", "loan"), 0, 0)
 
@@ -230,7 +226,7 @@
         out_specs=vmem,
         compiler_params=pltpu.CompilerParams(vmem_limit_bytes=16 << 20),
         name="second_pass",
-    )(shard, everyone, weighted, member, high, low)
+    )(shard, everyone, weighted, reach, high, low)
 
     return jnp.sum(lax.all_to_all(parts, ("tm", "loan"), 0, 0), axis=0)
 

time: 37.2 us -> 37 us (level)
  no operation moved by 1% of the time
where the time goes in v4:
time: 37 us; the launch traced here: 36.7 us
  blocking collectives  22.3 us (60%)
  Pallas kernels  7.77 us (21%)
  starting transfers between devices  3.03 us (8%)
  waiting for transfers between devices  2.25 us (6%)
  between operations  0.68 us (2%)
  other arithmetic  0.63 us (2%)
    all_to_all x1, blocking collectives, per_device(): everyone = lax.all_to_all(stats, ('tm', 'loan'), 0, 0)  13 us
    all_to_all x1, blocking collectives, per_device(): return jnp.sum(lax.all_to_all(parts, ('tm', 'loan'), 0, 0), axis=0)  9.31 us
    pallas_call x1, Pallas kernels, per_device(): pl.pallas_call(functools.partial(first_pass, chunk), out_shape=(arr((3, r...  5.05 us
    ppermute x1, starting transfers between devices, per_device(): other = lax.ppermute(lin, 'cov', pairs)  3.03 us
    ppermute x1, waiting for transfers between devices, per_device(): other = lax.ppermute(lin, 'cov', pairs)  2.25 us
    pallas_call x1, Pallas kernels, per_device(): pl.pallas_call(functools.partial(second_pass, shards, 1.0 / records), out...  1.99 us
  transfers between devices with their start and end apart: 1, of which 1 were waited for; matrix products, arithmetic and copies ran while one was open for 0% of the time, Pallas kernels for 0%

profile of v4, /device:TPU:0, one launch (start us, length us, event | category | flops | bytes accessed | tf_op | source)
XLA Modules:
  0.0 36.7 jit_solution(10858440208834554806)
XLA Ops:
  0.7 5.0 %first_pass.1 = (f32[3,4096]{1,0:T(4,128)S(1)}, f32[1,4096]{1,0:T(1,128)S(1)}, f32[1,4096]{1,0:T(1,128)S(1)}, bf16[256,4096]{1,0:T(8,128)(2,1)S(1)}, bf16[4096,5...) custom-call(f32[4096,512]{1,0:T(8,128)} %covars.1, s32[1,4096]{1,0:T(1,128)} %bitcast.4, s32[1,4096]{1,0:T(1,128)} %bitcast.5, ...), custom_call_target="tpu_custom_call" | custom-call | tf_op jit(solution)/shard_map/first_pass/pallas_call | solution.py:179
  5.7 3.0 %collective-permute-start = (f32[3,4096]{1,0:T(4,128)S(1)}, f32[3,4096]{1,0:T(4,128)S(1)}, u32[]{:S(2)}, u32[]{:S(2)}) collective-permute-start(f32[3,4096]{1,0:T(4,128)S(1)} %get-tuple-element.13.mine), channel_id=1, source_target_pairs={{0,1},{1,0},{2,3},{3,2},{4,5},{5,4},{6,7},{7,6},{8,9},{9,8},{10,11... | collective-permute-start | bytes 147464 | tf_op jit(solution)/shard_map/ppermute | solution.py:209
  8.7 2.2 %collective-permute-done.other = f32[3,4096]{1,0:T(4,128)S(1)} collective-permute-done((f32[3,4096]{1,0:T(4,128)S(1)}, f32[3,4096]{1,0:T(4,128)S(1)}, u32[]{:S(2)}, u32[]{:S(2)}) %collective-permute-start) | collective-permute-done | bytes 49184 | tf_op jit(solution)/shard_map/ppermute | solution.py:209
  11.0 0.7 %tally.1 = (f32[16,4,256]{2,1,0:T(4,128)S(1)}, f32[3,4096]{1,0:T(4,128)S(1)}) custom-call(f32[3,4096]{1,0:T(4,128)S(1)} %get-tuple-element.13.mine, f32[3,4096]{1,0:T(4,128)S(1)} %collective-permute-done.other, f32[1,4096]{1,0:T(1,128)S(1)} %get-tuple-element.14.valid, f32[1,4096]{1,0:T(1,128)S(1)} %get-tuple-element.15.died, ...), custom_call_target="tpu_custom_call" | custom-call | tf_op jit(solution)/shard_map/tally/pallas_call | solution.py:211
  11.7 13.0 %all_to_all.10.stats = f32[16,4,256]{2,1,0:T(4,128)S(1)} all-to-all(f32[16,4,256]{2,1,0:T(4,128)S(1)} %get-tuple-element.17), channel_id=1, replica_groups=mesh['tm'=2,'loan'=8,'cov'=2] {'tm','loan'}, dimensions={0} | all-to-all | bytes 131072 | tf_op jit(solution)/shard_map/all_to_all | solution.py:220
  24.8 2.0 %second_pass.1 = f32[16,2,512]{2,1,0:T(2,128)S(1)} custom-call(s32[1]{0:T(128)} %bitcast.shard, f32[16,4,256]{2,1,0:T(4,128)S(1)} %all_to_all.10.stats, f32[3,4096]{1,0:T(4,128)S(1)} %get-tuple-element.18.weighted, bf16[256,4096]{1,0:T(8,128)(2,1)S(1)} %get-tuple-element.16.reach, bf16[4096,512]{1,0:T(8,128)(2,1)S(1)} %get-tuple-element.19.high, ...), custom_call_target="tpu_custom_call" | custom-call | tf_op jit(solution)/shard_map/second_pass/pallas_call | solution.py:222
  26.8 9.3 %all_to_all.11 = f32[16,2,512]{2,1,0:T(2,128)S(1)} all-to-all(f32[16,2,512]{2,1,0:T(2,128)S(1)} %second_pass.1), channel_id=1, replica_groups=mesh['tm'=2,'loan'=8,'cov'=2] {'tm','loan'}, dimensions={0} | all-to-all | bytes 131072 | tf_op jit(solution)/shard_map/all_to_all | solution.py:231
  36.1 0.6 %reduce_sum.9 = f32[2,512]{1,0:T(2,128)} reduce(f32[16,2,512]{2,1,0:T(2,128)S(1)} %all_to_all.11, f32[]{:T(128)} %constant.7.clone.1), dimensions={0}, to_apply=%region_0.0 | reduce | flops 15360 | bytes 69636 | tf_op jit(solution)/shard_map/reduce_sum | solution.py:231
Async XLA Ops:
  5.7 5.3 %collective-permute-start = (f32[3,4096]{1,0:T(4,128)S(1)}, f32[3,4096]{1,0:T(4,128)S(1)}, u32[]{:S(2)}, u32[]{:S(2)}) collective-permute-start(f32[3,4096]{1,0:T(4,128)S(1)} %get-tuple-element.13.mine), channel_id=1, source_target_pairs={{0,1},{1,0},{2,3},{3,2},{4,5},{5,4},{6,7},{7,6},{8,9},{9,8},{10,11... | collective-permute-start | bytes 147464 | tf_op jit(solution)/shard_map/ppermute | solution.py:209

commit v5 on v4

--- a/solution.py
+++ b/solution.py
@@ -8,6 +8,7 @@
 from jax.sharding import PartitionSpec as P
 
 G_SH = 256
+LANES = 128
 BF16 = jnp.bfloat16
 F32 = jnp.float32
 
@@ -20,18 +21,13 @@
 
 
 def stack3(x):
-    hi, mid, low = split3(x)
-    return jnp.concatenate([hi, mid, low, jnp.zeros_like(x)], axis=0).astype(BF16)
-
-
-def unstack3(y):
-    return (y[16:24] + y[8:16]) + y[0:8]
-
-
-def pad8(rows):
-    width = rows[0].shape[1]
-    used = sum(r.shape[0] for r in rows)
-    return jnp.concatenate(list(rows) + [jnp.zeros((8 - used, width), F32)], axis=0)
+    used, width = x.shape
+    rest = jnp.zeros((16 - 3 * used, width), F32)
+    return jnp.concatenate([*split3(x), rest], axis=0).astype(BF16)
+
+
+def unstack3(y, used):
+    return (y[2 * used : 3 * used] + y[used : 2 * used]) + y[0:used]
 
 
 def first_pass(
@@ -59,11 +55,12 @@
         piece(1).start()
     for copy in copies:
         copy.wait()
-    index = lax.broadcasted_iota(jnp.int32, (1, rows), 1)
-    ok = index < counts[0]
+    dense = (rows // LANES, LANES)
+    index = lax.broadcasted_iota(jnp.int32, dense, 0) * LANES
+    ok = index + lax.broadcasted_iota(jnp.int32, dense, 1) < counts[0]
     valid[...] = jnp.where(ok, 1.0, 0.0)
     died[...] = jnp.where(ok, events_v[...].astype(F32), 0.0)
-    coeffs = stack3(pad8([beta_v[...], vecs_v[...]]))
+    coeffs = stack3(jnp.concatenate([beta_v[...], vecs_v[...]], axis=0))
     base = shard[0] * G_SH
     part = min(512, chunk)
 
@@ -94,23 +91,35 @@
         dims = (((1,), (1,)), ((), ()))
         out = lax.dot_general(coeffs, hi, dims, preferred_element_type=F32)
         out += lax.dot_general(coeffs, lo, dims, preferred_element_type=F32)
-        lin[:, at] = unstack3(out)[0:3]
+        values = unstack3(out, 3)
+        per = chunk // LANES
+        place = lin.at[:, pl.ds(pl.multiple_of(step * per, per), per)]
+        for j in range(per):
+            place[:, j, :] = values[:, j * LANES : (j + 1) * LANES]
         return carry
 
     lax.fori_loop(0, steps, body, 0)
 
 
-def tally(mine, other, valid, died, reach, stats, weighted):
+def tally(mine, other, valid, died, reach, stats, weighted, spread, keep):
     total = mine[...] + other[...]
-    weight = jnp.where(valid[...] > 0.0, jnp.exp(total[0:1]), 0.0)
-    proj = total[1:3]
-    weighted[0:1] = weight
-    weighted[1:3] = proj
-    rows = pad8([weight, weight * proj, died[...]])
+    weight = jnp.where(valid[...] > 0.0, jnp.exp(total[0]), 0.0)
+    values = (weight, weight * total[1], weight * total[2], died[...])
+    keep[0] = weight
+    keep[1] = total[1]
+    keep[2] = total[2]
+    for k, value in enumerate(values):
+        for part, piece in enumerate(split3(value)):
+            spread[4 * part + k] = piece
+        spread[12 + k] = jnp.zeros_like(value)
+    steps = weight.shape[0]
+    for j in range(steps):
+        weighted[:, j * LANES : (j + 1) * LANES] = keep[:, j, :]
+    lhs = jnp.concatenate([spread[:, j, :] for j in range(steps)], axis=1).astype(BF16)
     out = lax.dot_general(
-        stack3(rows), reach[...], (((1,), (1,)), ((), ())), preferred_element_type=F32
+        lhs, reach[...], (((1,), (1,)), ((), ())), preferred_element_type=F32
     )
-    sums = unstack3(out)[0:4]
+    sums = unstack3(out, 4)
     for slot in range(stats.shape[0]):
         stats[slot] = sums
 
@@ -139,22 +148,22 @@
         late = per_shard[s][3:4]
         died_grp = late - jnp.where(lane == width - 1, 0.0, pltpu.roll(late, width - 1, 1))
         risk0 = risk[0:1]
-        return pad8([died_grp / risk0, died_grp * risk[1:3] / (risk0 * risk0)])
-
-    chosen = jnp.zeros((8, width), F32)
-    head = jnp.zeros((8, 1), F32)
+        return jnp.concatenate([died_grp / risk0, died_grp * risk[1:3] / (risk0 * risk0)], axis=0)
+
+    chosen = jnp.zeros((3, width), F32)
+    head = jnp.zeros((3, 1), F32)
     for s in range(shards):
         value = ratios_of(s)
         chosen = jnp.where(me == s, value, chosen)
         head = head + jnp.where(me > s, jnp.sum(value, axis=1, keepdims=True), 0.0)
-    looked = unstack3(jnp.dot(stack3(chosen), reach[...], preferred_element_type=F32)) + head
+    looked = unstack3(jnp.dot(stack3(chosen), reach[...], preferred_element_type=F32), 3) + head
     weight = weighted[0:1]
     proj = weighted[1:3]
     resid = weight * (proj * looked[0:1] - looked[1:3])
-    lhs = stack3(pad8([resid]))
+    lhs = stack3(resid)
     prod = jnp.dot(lhs, high[...], preferred_element_type=F32)
     prod += jnp.dot(lhs, low[...], preferred_element_type=F32)
-    prod = unstack3(prod)[0:2] * scale
+    prod = unstack3(prod, 2) * scale
     for slot in range(out.shape[0]):
         out[slot] = prod
 
@@ -165,6 +174,7 @@
     peers = shards * lax.axis_size("loan")
     records = rows * peers
     chunk = min(1024, rows)
+    dense = (rows // LANES, LANES)
     shard = lax.axis_index("tm").astype(jnp.int32)[None]
     hbm = pl.BlockSpec(memory_space=pltpu.HBM)
     vmem = pl.BlockSpec(memory_space=pltpu.VMEM)
@@ -179,7 +189,7 @@
     lin, died, valid, reach, high, low = pl.pallas_call(
         functools.partial(first_pass, chunk),
         out_shape=(
-            arr((3, rows)), arr((1, rows)), arr((1, rows)),
+            arr((3, *dense)), arr(dense), arr(dense),
             kept((G_SH, rows), BF16), kept((rows, cols), BF16), kept((rows, cols), BF16),
         ),
         in_specs=[hbm] * 3 + [smem] * 2 + [hbm] * 2,
@@ -189,7 +199,7 @@
             pltpu.VMEM((1, cols), F32),
             pltpu.VMEM((2, cols), F32),
             pltpu.VMEM((1, rows), jnp.int32),
-            pltpu.VMEM((1, rows), jnp.int32),
+            pltpu.VMEM(dense, jnp.int32),
             pltpu.SemaphoreType.DMA((rows // chunk,)),
             pltpu.SemaphoreType.DMA((4,)),
         ],
@@ -198,7 +208,7 @@
     )(
         *(
             pltpu.with_memory_space_constraint(x, pltpu.HBM)
-            for x in (covars, events[None], group[None])
+            for x in (covars, events.reshape(dense), group[None])
         ),
         counts,
         shard,
@@ -213,6 +223,7 @@
         out_shape=(arr((peers, 4, G_SH)), arr((3, rows))),
         in_specs=[vmem] * 5,
         out_specs=(vmem,) * 2,
+        scratch_shapes=[pltpu.VMEM((16, *dense), F32), pltpu.VMEM((3, *dense), F32)],
         compiler_params=pltpu.CompilerParams(vmem_limit_bytes=16 << 20),
         name="tally",
     )(lin, other, valid, died, reach)

time: 37 us -> 36.2 us (0.978)
  Pallas kernels: 7.77 us -> 7.15 us
    pallas_call x1, Pallas kernels: 1.99 us -> 1.55 us  [per_device(): pl.pallas_call(functools.partial(second_pass, shards, 1.0 / records), out...]
where the time goes in v5:
time: 36.2 us; the launch traced here: 35.9 us
  blocking collectives  22.3 us (62%)
  Pallas kernels  7.15 us (20%)
  starting transfers between devices  3.03 us (8%)
  waiting for transfers between devices  2.07 us (6%)
  between operations  0.68 us (2%)
  other arithmetic  0.63 us (2%)
    all_to_all x1, blocking collectives, per_device(): everyone = lax.all_to_all(stats, ('tm', 'loan'), 0, 0)  13 us
    all_to_all x1, blocking collectives, per_device(): return jnp.sum(lax.all_to_all(parts, ('tm', 'loan'), 0, 0), axis=0)  9.31 us
    pallas_call x1, Pallas kernels, per_device(): pl.pallas_call(functools.partial(first_pass, chunk), out_shape=(arr((3, *...  4.89 us
    ppermute x1, starting transfers between devices, per_device(): other = lax.ppermute(lin, 'cov', pairs)  3.03 us
    ppermute x1, waiting for transfers between devices, per_device(): other = lax.ppermute(lin, 'cov', pairs)  2.07 us
    pallas_call x1, Pallas kernels, per_device(): pl.pallas_call(functools.partial(second_pass, shards, 1.0 / records), out...  1.55 us
  transfers between devices with their start and end apart: 1, of which 1 were waited for; matrix products, arithmetic and copies ran while one was open for 0% of the time, Pallas kernels for 0%

profile of v5, /device:TPU:0, one launch (start us, length us, event | category | flops | bytes accessed | tf_op | source)
XLA Modules:
  0.0 35.9 jit_solution(15516796957063875432)
XLA Ops:
  0.7 4.9 %first_pass.1 = (f32[3,32,128]{2,1,0:T(8,128)S(1)}, f32[32,128]{1,0:T(8,128)S(1)}, f32[32,128]{1,0:T(8,128)S(1)}, bf16[256,4096]{1,0:T(8,128)(2,1)S(1)}, bf16[40...) custom-call(f32[4096,512]{1,0:T(8,128)} %covars.1, s32[32,128]{1,0:T(8,128)} %bitcast.4, s32[1,4096]{1,0:T(1,128)} %bitcast.5, ...), custom_call_target="tpu_custom_call" | custom-call | tf_op jit(solution)/shard_map/first_pass/pallas_call | solution.py:189
  5.5 3.0 %collective-permute-start = (f32[3,32,128]{2,1,0:T(8,128)S(1)}, f32[3,32,128]{2,1,0:T(8,128)S(1)}, u32[]{:S(2)}, u32[]{:S(2)}) collective-permute-start(f32[3,32,128]{2,1,0:T(8,128)S(1)} %get-tuple-element.13.mine), channel_id=1, source_target_pairs={{0,1},{1,0},{2,3},{3,2},{4,5},{5,4},{6,7},{7,6},{8,9},{9,8},{10,11... | collective-permute-start | bytes 147464 | tf_op jit(solution)/shard_map/ppermute | solution.py:219
  8.6 2.1 %collective-permute-done.other = f32[3,32,128]{2,1,0:T(8,128)S(1)} collective-permute-done((f32[3,32,128]{2,1,0:T(8,128)S(1)}, f32[3,32,128]{2,1,0:T(8,128)S(1)}, u32[]{:S(2)}, u32[]{:S(2)}) %collective-permute-start) | collective-permute-done | bytes 49184 | tf_op jit(solution)/shard_map/ppermute | solution.py:219
  10.6 0.7 %tally.1 = (f32[16,4,256]{2,1,0:T(4,128)S(1)}, f32[3,4096]{1,0:T(4,128)S(1)}) custom-call(f32[3,32,128]{2,1,0:T(8,128)S(1)} %get-tuple-element.13.mine, f32[3,32,128]{2,1,0:T(8,128)S(1)} %collective-permute-done.other, f32[32,128]{1,0:T(8,128)S(1)} %get-tuple-element.14.valid, f32[32,128]{1,0:T(8,128)S(1)} %get-tuple-element.15.died, ...), custom_call_target="tpu_custom_call" | custom-call | tf_op jit(solution)/shard_map/tally/pallas_call | solution.py:221
  11.4 13.0 %all_to_all.10.stats = f32[16,4,256]{2,1,0:T(4,128)S(1)} all-to-all(f32[16,4,256]{2,1,0:T(4,128)S(1)} %get-tuple-element.17), channel_id=1, replica_groups=mesh['tm'=2,'loan'=8,'cov'=2] {'tm','loan'}, dimensions={0} | all-to-all | bytes 131072 | tf_op jit(solution)/shard_map/all_to_all | solution.py:231
  24.4 1.5 %second_pass.1 = f32[16,2,512]{2,1,0:T(2,128)S(1)} custom-call(s32[1]{0:T(128)} %bitcast.shard, f32[16,4,256]{2,1,0:T(4,128)S(1)} %all_to_all.10.stats, f32[3,4096]{1,0:T(4,128)S(1)} %get-tuple-element.18.weighted, bf16[256,4096]{1,0:T(8,128)(2,1)S(1)} %get-tuple-element.16.reach, bf16[4096,512]{1,0:T(8,128)(2,1)S(1)} %get-tuple-element.19.high, ...), custom_call_target="tpu_custom_call" | custom-call | tf_op jit(solution)/shard_map/second_pass/pallas_call | solution.py:233
  26.0 9.3 %all_to_all.11 = f32[16,2,512]{2,1,0:T(2,128)S(1)} all-to-all(f32[16,2,512]{2,1,0:T(2,128)S(1)} %second_pass.1), channel_id=1, replica_groups=mesh['tm'=2,'loan'=8,'cov'=2] {'tm','loan'}, dimensions={0} | all-to-all | bytes 131072 | tf_op jit(solution)/shard_map/all_to_all | solution.py:242
  35.3 0.6 %reduce_sum.9 = f32[2,512]{1,0:T(2,128)} reduce(f32[16,2,512]{2,1,0:T(2,128)S(1)} %all_to_all.11, f32[]{:T(128)} %constant.7.clone.1), dimensions={0}, to_apply=%region_0.0 | reduce | flops 15360 | bytes 69636 | tf_op jit(solution)/shard_map/reduce_sum | solution.py:242
Async XLA Ops:
  5.5 5.1 %collective-permute-start = (f32[3,32,128]{2,1,0:T(8,128)S(1)}, f32[3,32,128]{2,1,0:T(8,128)S(1)}, u32[]{:S(2)}, u32[]{:S(2)}) collective-permute-start(f32[3,32,128]{2,1,0:T(8,128)S(1)} %get-tuple-element.13.mine), channel_id=1, source_target_pairs={{0,1},{1,0},{2,3},{3,2},{4,5},{5,4},{6,7},{7,6},{8,9},{9,8},{10,11... | collective-permute-start | bytes 147464 | tf_op jit(solution)/shard_map/ppermute | solution.py:219

commit v6 on v5

--- a/solution.py
+++ b/solution.py
@@ -51,6 +51,7 @@
         return pltpu.make_async_copy(covars.at[at], buf.at[at], sems.at[step])
 
     piece(0).start()
+    pl.delay(500)
     if steps > 1:
         piece(1).start()
     for copy in copies:
@@ -72,16 +73,16 @@
         return carry
 
     lax.fori_loop(0, rows // part, mark, 0)
-    if steps > 2:
-        piece(2).start()
+    for step in range(2, min(4, steps)):
+        piece(step).start()
 
     def body(step, carry):
         at = pl.ds(pl.multiple_of(step * chunk, chunk), chunk)
         piece(step).wait()
 
-        @pl.when(step + 3 < steps)
+        @pl.when(step + 4 < steps)
         def _():
-            piece(step + 3).start()
+            piece(step + 4).start()
 
         full = buf[at, :]
         hi = full.astype(BF16)

time: 36.2 us -> 35.9 us (level)
  no operation moved by 1% of the time
where the time goes in v6:
time: 35.9 us; the launch traced here: 35.6 us
  blocking collectives  22.3 us (62%)
  Pallas kernels  6.86 us (19%)
  starting transfers between devices  3.03 us (8%)
  waiting for transfers between devices  2.07 us (6%)
  between operations  0.68 us (2%)
  other arithmetic  0.63 us (2%)
    all_to_all x1, blocking collectives, per_device(): everyone = lax.all_to_all(stats, ('tm', 'loan'), 0, 0)  13 us
    all_to_all x1, blocking collectives, per_device(): return jnp.sum(lax.all_to_all(parts, ('tm', 'loan'), 0, 0), axis=0)  9.31 us
    pallas_call x1, Pallas kernels, per_device(): pl.pallas_call(functools.partial(first_pass, chunk), out_shape=(arr((3, *...  4.59 us
    ppermute x1, starting transfers between devices, per_device(): other = lax.ppermute(lin, 'cov', pairs)  3.03 us
    ppermute x1, waiting for transfers between devices, per_device(): other = lax.ppermute(lin, 'cov', pairs)  2.07 us
    pallas_call x1, Pallas kernels, per_device(): pl.pallas_call(functools.partial(second_pass, shards, 1.0 / records), out...  1.55 us
    pallas_call x1, Pallas kernels, per_device(): pl.pallas_call(tally, out_shape=(arr((peers, 4, G_SH)), arr((3, rows))),...  0.72 us
  transfers between devices with their start and end apart: 1, of which 1 were waited for; matrix products, arithmetic and copies ran while one was open for 0% of the time, Pallas kernels for 0%

profile of v6, /device:TPU:0, one launch (start us, length us, event | category | flops | bytes accessed | tf_op | source)
XLA Modules:
  0.0 35.6 jit_solution(11903812398267045727)
XLA Ops:
  0.7 4.6 %first_pass.1 = (f32[3,32,128]{2,1,0:T(8,128)S(1)}, f32[32,128]{1,0:T(8,128)S(1)}, f32[32,128]{1,0:T(8,128)S(1)}, bf16[256,4096]{1,0:T(8,128)(2,1)S(1)}, bf16[40...) custom-call(f32[4096,512]{1,0:T(8,128)} %covars.1, s32[32,128]{1,0:T(8,128)} %bitcast.4, s32[1,4096]{1,0:T(1,128)} %bitcast.5, ...), custom_call_target="tpu_custom_call" | custom-call | tf_op jit(solution)/shard_map/first_pass/pallas_call | solution.py:190
  5.3 3.0 %collective-permute-start = (f32[3,32,128]{2,1,0:T(8,128)S(1)}, f32[3,32,128]{2,1,0:T(8,128)S(1)}, u32[]{:S(2)}, u32[]{:S(2)}) collective-permute-start(f32[3,32,128]{2,1,0:T(8,128)S(1)} %get-tuple-element.13.mine), channel_id=1, source_target_pairs={{0,1},{1,0},{2,3},{3,2},{4,5},{5,4},{6,7},{7,6},{8,9},{9,8},{10,11... | collective-permute-start | bytes 147464 | tf_op jit(solution)/shard_map/ppermute | solution.py:220
  8.3 2.1 %collective-permute-done.other = f32[3,32,128]{2,1,0:T(8,128)S(1)} collective-permute-done((f32[3,32,128]{2,1,0:T(8,128)S(1)}, f32[3,32,128]{2,1,0:T(8,128)S(1)}, u32[]{:S(2)}, u32[]{:S(2)}) %collective-permute-start) | collective-permute-done | bytes 49184 | tf_op jit(solution)/shard_map/ppermute | solution.py:220
  10.4 0.7 %tally.1 = (f32[16,4,256]{2,1,0:T(4,128)S(1)}, f32[3,4096]{1,0:T(4,128)S(1)}) custom-call(f32[3,32,128]{2,1,0:T(8,128)S(1)} %get-tuple-element.13.mine, f32[3,32,128]{2,1,0:T(8,128)S(1)} %collective-permute-done.other, f32[32,128]{1,0:T(8,128)S(1)} %get-tuple-element.14.valid, f32[32,128]{1,0:T(8,128)S(1)} %get-tuple-element.15.died, ...), custom_call_target="tpu_custom_call" | custom-call | tf_op jit(solution)/shard_map/tally/pallas_call | solution.py:222
  11.1 13.0 %all_to_all.10.stats = f32[16,4,256]{2,1,0:T(4,128)S(1)} all-to-all(f32[16,4,256]{2,1,0:T(4,128)S(1)} %get-tuple-element.17), channel_id=1, replica_groups=mesh['tm'=2,'loan'=8,'cov'=2] {'tm','loan'}, dimensions={0} | all-to-all | bytes 131072 | tf_op jit(solution)/shard_map/all_to_all | solution.py:232
  24.1 1.5 %second_pass.1 = f32[16,2,512]{2,1,0:T(2,128)S(1)} custom-call(s32[1]{0:T(128)} %bitcast.shard, f32[16,4,256]{2,1,0:T(4,128)S(1)} %all_to_all.10.stats, f32[3,4096]{1,0:T(4,128)S(1)} %get-tuple-element.18.weighted, bf16[256,4096]{1,0:T(8,128)(2,1)S(1)} %get-tuple-element.16.reach, bf16[4096,512]{1,0:T(8,128)(2,1)S(1)} %get-tuple-element.19.high, ...), custom_call_target="tpu_custom_call" | custom-call | tf_op jit(solution)/shard_map/second_pass/pallas_call | solution.py:234
  25.7 9.3 %all_to_all.11 = f32[16,2,512]{2,1,0:T(2,128)S(1)} all-to-all(f32[16,2,512]{2,1,0:T(2,128)S(1)} %second_pass.1), channel_id=1, replica_groups=mesh['tm'=2,'loan'=8,'cov'=2] {'tm','loan'}, dimensions={0} | all-to-all | bytes 131072 | tf_op jit(solution)/shard_map/all_to_all | solution.py:243
  35.0 0.6 %reduce_sum.9 = f32[2,512]{1,0:T(2,128)} reduce(f32[16,2,512]{2,1,0:T(2,128)S(1)} %all_to_all.11, f32[]{:T(128)} %constant.7.clone.1), dimensions={0}, to_apply=%region_0.0 | reduce | flops 15360 | bytes 69636 | tf_op jit(solution)/shard_map/reduce_sum | solution.py:243
Async XLA Ops:
  5.3 5.1 %collective-permute-start = (f32[3,32,128]{2,1,0:T(8,128)S(1)}, f32[3,32,128]{2,1,0:T(8,128)S(1)}, u32[]{:S(2)}, u32[]{:S(2)}) collective-permute-start(f32[3,32,128]{2,1,0:T(8,128)S(1)} %get-tuple-element.13.mine), channel_id=1, source_target_pairs={{0,1},{1,0},{2,3},{3,2},{4,5},{5,4},{6,7},{7,6},{8,9},{9,8},{10,11... | collective-permute-start | bytes 147464 | tf_op jit(solution)/shard_map/ppermute | solution.py:220
